TPU v7x, 256 devices: a whole 4x4x8 slice. The times are simulated.
256 devices in a mesh: gx: 64 (over z, x, core), gy: 4 (over y).
Axes of the slice: x: 4, y: 4, z: 8, core: 2. Of those that a mesh axis runs over, the one named last changes fastest.
Arguments:
- pressure: float32 [512, 512, 128], P('gx', 'gy'), may hold values from -6 to 8
- vel_y: float32 [512, 512, 128], P('gx', 'gy'), may hold values from -6 to 6
- vel_z: float32 [512, 512, 128], P('gx', 'gy'), may hold values from -6 to 6
- material: int32 [512, 512, 128], P('gx', 'gy'), may hold values from 0 to 7
- absorb_table: float32 [8], replicated, may hold values from 0.02 to 4
Outputs:
- pressure_next: float32 [512, 512, 128], P('gx', 'gy')
- vel_y_next: float32 [512, 512, 128], P('gx', 'gy')
- vel_z_next: float32 [512, 512, 128], P('gx', 'gy')
All inputs are finite; a program needn't handle non-finite values.
Results may differ from a plain program's by a relative error of at most 0.0004.
Values sent between devices are 32-bit elements; how exact they have to be, the bound alone decides.
A program may use at most 128 MiB of HBM per device.

v0:
```python
import jax
import jax.numpy as jnp
from jax import lax
from jax.sharding import PartitionSpec as P

MATS = 8


def passed_along(value, axis, steps):
    count = lax.axis_size(axis)
    first, last = (max(0, -steps), min(count, count - steps))
    return lax.ppermute(value, axis, [(source, source + steps) for source in range(first, last)])


def join_segments(left, right):
    denom = 1.0 - left[5] * right[1]
    inner_const = (left[3] + left[5] * right[0]) / denom
    inner_left = left[4] / denom
    inner_right = left[5] * right[2] / denom
    outer_const = right[0] + right[1] * inner_const
    outer_left = right[1] * inner_left
    outer_right = right[2] + right[1] * inner_right
    return (
        left[0] + left[2] * outer_const,
        left[1] + left[2] * outer_left,
        left[2] * outer_right,
        right[3] + right[4] * inner_const,
        right[4] * inner_left,
        right[5] + right[4] * inner_right,
    )


def sweep_lines(excess, stacked):

    def forward(carry, items):
        carried, value_prev = carry
        excess_row, value_row = items
        inverse = 1.0 / (1.0 + excess_row + carried)
        value = (value_row + value_prev) * inverse[None]
        carried_next = (excess_row + carried) * inverse
        return ((carried_next, value), (inverse, value))

    start = (jnp.ones(excess.shape[1:], jnp.float32), jnp.zeros(stacked.shape[1:], jnp.float32))
    _, (inverses, values) = lax.scan(forward, start, (excess, stacked))

    def backward(following, items):
        inverse, value = items
        current = value + inverse[None] * following
        return (current, current)

    _, solved = lax.scan(
        backward, jnp.zeros(stacked.shape[1:], jnp.float32), (inverses, values), reverse=True
    )
    return solved


def body(pressure, vel_y, vel_z, material, absorb_table):
    absorb = jnp.zeros(pressure.shape, jnp.float32)
    for entry in range(MATS):
        absorb = absorb + jnp.where(material == entry, absorb_table[entry], 0.0)
    damping = 1.0 / (1.0 + absorb)
    above = passed_along(pressure[:, :1, :], "gy", -1)
    upper_y = jnp.concatenate([pressure[:, 1:, :], above], axis=1)
    upper_z = jnp.concatenate([pressure[:, :, 1:], jnp.zeros_like(pressure[:, :, :1])], axis=2)
    vel_y_next = damping * (vel_y - 0.5 * (upper_y - pressure))
    vel_z_next = damping * (vel_z - 0.5 * (upper_z - pressure))
    below = passed_along(vel_y_next[:, -1:, :], "gy", 1)
    lower_y = jnp.concatenate([below, vel_y_next[:, :-1, :]], axis=1)
    lower_z = jnp.concatenate([jnp.zeros_like(pressure[:, :, :1]), vel_z_next[:, :, :-1]], axis=2)
    source = pressure - 0.5 * (vel_y_next - lower_y + vel_z_next - lower_z)
    line_cells = pressure.shape[0] * lax.axis_size("gx")
    coupling = 1.0 * (line_cells * line_cells // 4)
    excess = (1.0 + absorb) / coupling
    scaled = source / coupling
    rows = lax.broadcasted_iota(jnp.int32, pressure.shape, 0)
    first_unit = jnp.where(rows == 0, -1.0, 0.0)
    last_unit = jnp.where(rows == pressure.shape[0] - 1, -1.0, 0.0)
    stacked = jnp.stack([scaled, first_unit, last_unit], axis=1)
    solved = sweep_lines(excess, stacked)
    local_part = solved[:, 0]
    left_spike = solved[:, 1]
    right_spike = solved[:, 2]
    own = (
        local_part[0],
        -left_spike[0],
        -right_spike[0],
        local_part[-1],
        -left_spike[-1],
        -right_spike[-1],
    )
    nothing = jnp.zeros(local_part.shape[1:], jnp.float32)
    single = jnp.ones(local_part.shape[1:], jnp.float32)
    identity = (nothing, nothing, single, nothing, single, nothing)
    table = (
        lax.all_gather(own[0][None], "gx", axis=0, tiled=True),
        lax.all_gather(own[1][None], "gx", axis=0, tiled=True),
        lax.all_gather(own[2][None], "gx", axis=0, tiled=True),
        lax.all_gather(own[3][None], "gx", axis=0, tiled=True),
        lax.all_gather(own[4][None], "gx", axis=0, tiled=True),
        lax.all_gather(own[5][None], "gx", axis=0, tiled=True),
    )
    position = lax.axis_index("gx")
    indices = jnp.arange(lax.axis_size("gx"), dtype=jnp.int32)

    def take_lower(carry, items):
        index, pieces = items
        merged = join_segments(carry, pieces)
        keep = index < position
        return (tuple((jnp.where(keep, fresh, older) for fresh, older in zip(merged, carry))), None)

    def take_higher(carry, items):
        index, pieces = items
        merged = join_segments(pieces, carry)
        keep = index > position
        return (tuple((jnp.where(keep, fresh, older) for fresh, older in zip(merged, carry))), None)

    prefix, _ = lax.scan(take_lower, identity, (indices, table))
    suffix, _ = lax.scan(take_higher, identity, (indices, table), reverse=True)
    top_rhs = own[0] + own[1] * prefix[3] + own[2] * suffix[0]
    bottom_rhs = own[3] + own[4] * prefix[3] + own[5] * suffix[0]
    top_top = 1.0 - own[1] * prefix[5]
    top_bottom = -own[2] * suffix[1]
    bottom_top = -own[4] * prefix[5]
    bottom_bottom = 1.0 - own[5] * suffix[1]
    determinant = top_top * bottom_bottom - top_bottom * bottom_top
    top_value = (top_rhs * bottom_bottom - top_bottom * bottom_rhs) / determinant
    bottom_value = (top_top * bottom_rhs - bottom_top * top_rhs) / determinant
    before_value = prefix[3] + prefix[5] * top_value
    after_value = suffix[0] + suffix[1] * bottom_value
    pressure_next = local_part - left_spike * before_value[None] - right_spike * after_value[None]
    return (pressure_next, vel_y_next, vel_z_next)


def solution(mesh):
    return jax.shard_map(
        body,
        mesh=mesh,
        in_specs=(
            P("gx", "gy", None),
            P("gx", "gy", None),
            P("gx", "gy", None),
            P("gx", "gy", None),
            P(),
        ),
        out_specs=(P("gx", "gy", None), P("gx", "gy", None), P("gx", "gy", None)),
        check_vma=False,
    )
```

profile of v0, /device:TPU:1, one launch (start us, length us, event | category | flops | bytes accessed | tf_op | source)
XLA Modules:
  0.0 848.9 jit_solution(11246831425350953470)
XLA Ops:
  8.1 1.3 collective-permute-start
  9.4 1.6 fusion.49
  11.0 1.1 slice.93
  12.1 1.2 slice.97
  13.4 6.4 fusion.32
  19.8 4.6 collective-permute-start.1
  25.8 1.4 broadcast.68.clone
  27.2 20.3 %while.64 = (s32[]{:T(128)}, f32[128,128]{1,0:T(8,128)S(1)}, f32[3,128,128]{2,1,0:T(8,128)S(1)}, f32[8,128,128]{2,1,0:T(8,128)S(1)}, f32[8,3,128,128]{3,2,1,0:T(...) while((s32[]{:T(128)}, f32[128,128]{1,0:T(8,128)S(1)}, ...), condition=%wide.region_1.2_spmd.clone, body=%wide.region_0.1_spmd.clone.sunk | while | flops 262147 | bytes 1376881 | solution.py:44
  48.5 15.2 %while.65 = (s32[]{:T(128)}, f32[3,128,128]{2,1,0:T(8,128)S(1)}, f32[8,3,128,128]{3,2,1,0:T(8,128)S(1)}, f32[8,3,128,128]{3,2,1,0:T(8,128)}, f32[8,128,128]{2,1,0:T(8,128)}, /*index=5*/s32[]{:T(128)}, s32[]{:T(128)}, s32[]{:T(128)}) while((s32[]{:T(128)}, f32[3,128,128]{2,1,0:T(8,128)S(1)}, f32[8,3,128,128]{3,2,1,0:T(8,128)S(1)}, ...), condition=%wide.region_3.4_spmd.clone, body=%wide.region_2.3_spmd.clone.sunk | while | flops 147460 | bytes 983155 | solution.py:51
  67.7 81.3 %all-gather.13.cloned.1.call-done = f32[64,1,128,128]{3,2,1,0:T(8,128)} async-done(((f32[1,1,128,128]{3,2,1,0:T(8,128)}), f32[64,1,128,128]{3,2,1,0:T(8,128)}) %all-gather.13.cloned.1.call-update) | async-done | bytes 4194320 | tf_op jit(solution)/shard_map/all_gather | solution.py:98
  149.1 79.5 %all-gather.15.cloned.1.call-done = f32[64,1,128,128]{3,2,1,0:T(8,128)} async-done(((f32[1,1,128,128]{3,2,1,0:T(8,128)}), f32[64,1,128,128]{3,2,1,0:T(8,128)}) %all-gather.15.cloned.1.call-update) | async-done | bytes 4194320 | tf_op jit(solution)/shard_map/all_gather | solution.py:99
  228.6 79.0 %all-gather.17.cloned.1.call-done = f32[64,1,128,128]{3,2,1,0:T(8,128)} async-done(((f32[1,1,128,128]{3,2,1,0:T(8,128)}), f32[64,1,128,128]{3,2,1,0:T(8,128)}) %all-gather.17.cloned.1.call-update) | async-done | bytes 4194320 | tf_op jit(solution)/shard_map/all_gather | solution.py:95
  307.6 78.8 %all-gather.19.cloned.1.call-done = f32[64,1,128,128]{3,2,1,0:T(8,128)} async-done(((f32[1,1,128,128]{3,2,1,0:T(8,128)}), f32[64,1,128,128]{3,2,1,0:T(8,128)}) %all-gather.19.cloned.1.call-update) | async-done | bytes 4194320 | tf_op jit(solution)/shard_map/all_gather | solution.py:96
  386.4 78.8 %all-gather.21.cloned.1.call-done = f32[64,1,128,128]{3,2,1,0:T(8,128)} async-done(((f32[1,1,128,128]{3,2,1,0:T(8,128)}), f32[64,1,128,128]{3,2,1,0:T(8,128)}) %all-gather.21.cloned.1.call-update) | async-done | bytes 4194320 | tf_op jit(solution)/shard_map/all_gather | solution.py:100
  465.2 78.8 %all-gather.23.cloned.1.call-done = f32[64,1,128,128]{3,2,1,0:T(8,128)} async-done(((f32[1,1,128,128]{3,2,1,0:T(8,128)}), f32[64,1,128,128]{3,2,1,0:T(8,128)}) %all-gather.23.cloned.1.call-update) | async-done | bytes 4194320 | tf_op jit(solution)/shard_map/all_gather | solution.py:97
  544.0 148.7 %while.67 = (s32[]{:T(128)}, f32[128,128]{1,0:T(8,128)S(1)}, f32[128,128]{1,0:T(8,128)S(1)}, s32[64]{0:T(128)S(1)}, s32[]{:T(128)}, /*index=5*/f32[64,128,128]{2...) while((s32[]{:T(128)}, f32[128,128]{1,0:T(8,128)S(1)}, ...), condition=%wide.region_7.8_spmd.clone, body=%wide.region_6.7_spmd.clone.sunk | while | flops 278533 | bytes 655541 | solution.py:118
  545.3 1.1 fusion.56
  547.6 1.1 fusion.56
  549.9 1.1 fusion.56
  552.3 1.1 fusion.56
  554.6 1.1 fusion.56
  556.9 1.1 fusion.56
  559.2 1.1 fusion.56
  561.5 1.1 fusion.56
  563.9 1.1 fusion.56
  566.2 1.1 fusion.56
  568.5 1.1 fusion.56
  570.8 1.1 fusion.56
  573.2 1.1 fusion.56
  575.5 1.1 fusion.56
  577.8 1.1 fusion.56
  692.7 148.3 %while.66 = (s32[]{:T(128)}, f32[128,128]{1,0:T(8,128)S(1)}, f32[128,128]{1,0:T(8,128)S(1)}, s32[64]{0:T(128)S(1)}, s32[]{:T(128)}, /*index=5*/f32[64,128,128]{2...) while((s32[]{:T(128)}, f32[128,128]{1,0:T(8,128)S(1)}, ...), condition=%wide.region_5.6_spmd.clone, body=%wide.region_4.5_spmd.clone.sunk | while | flops 245764 | bytes 655521 | solution.py:117
  (331 shorter events, 237.9 us)
Async XLA Ops:
  7.2 6.2 copy-start
  7.2 6.2 copy-start.4
  7.2 6.2 copy-start.5
  7.2 141.9 %all-gather.13.cloned.1.call-start = ((), (), s32[]{:S(2)}) async-start(), calls=%async_computation | async-start | bytes 4259840 | tf_op jit(solution)/shard_map/all_gather | solution.py:98
  7.2 6.2 copy-start.6
  8.1 5.2 collective-permute-start
  19.8 5.7 copy-start.1
  19.8 5.7 copy-start.2
  19.8 5.4 collective-permute-start.1
  47.5 0.8 copy-start.3
  64.5 164.2 %all-gather.15.cloned.1.call-start = ((), (), s32[]{:S(2)}) async-start(), calls=%async_computation.1 | async-start | bytes 4259840 | tf_op jit(solution)/shard_map/all_gather | solution.py:99
  65.2 242.4 %all-gather.17.cloned.1.call-start = ((), (), s32[]{:S(2)}) async-start(), calls=%async_computation.2 | async-start | bytes 4259840 | tf_op jit(solution)/shard_map/all_gather | solution.py:95
  65.9 320.5 %all-gather.19.cloned.1.call-start = ((), (), s32[]{:S(2)}) async-start(), calls=%async_computation.3 | async-start | bytes 4259840 | tf_op jit(solution)/shard_map/all_gather | solution.py:96
  66.5 398.7 %all-gather.21.cloned.1.call-start = ((), (), s32[]{:S(2)}) async-start(), calls=%async_computation.4 | async-start | bytes 4259840 | tf_op jit(solution)/shard_map/all_gather | solution.py:100
  67.1 476.9 %all-gather.23.cloned.1.call-start = ((), (), s32[]{:S(2)}) async-start(), calls=%async_computation.5 | async-start | bytes 4259840 | tf_op jit(solution)/shard_map/all_gather | solution.py:97
Sparse Core Ops, SparseCore 0:
  64.6 84.4 all-gather.12
  152.4 76.1 all-gather.14
  231.4 76.1 all-gather.16
  310.2 76.1 all-gather.18
  389.0 76.1 all-gather.20
  467.8 76.1 all-gather.22
where the time goes:
time: 859 us; the launch traced here: 849 us
  waiting for transfers between devices  480 us (56%)
  other arithmetic  172 us (20%)
  local copies, waits for them, and re-layouts  89.3 us (10%)
  loops' own time  86.8 us (10%)
  between operations  14.4 us (2%)
    all_gather x1, waiting for transfers between devices, body(): lax.all_gather(own[3][None], 'gx', axis=0, tiled=True)  81.3 us
    all_gather x1, waiting for transfers between devices, body(): lax.all_gather(own[4][None], 'gx', axis=0, tiled=True)  79.5 us
    all_gather x1, waiting for transfers between devices, body(): lax.all_gather(own[0][None], 'gx', axis=0, tiled=True)  79 us
    all_gather x1, waiting for transfers between devices, body(): lax.all_gather(own[2][None], 'gx', axis=0, tiled=True)  78.8 us
    all_gather x1, waiting for transfers between devices, body(): lax.all_gather(own[1][None], 'gx', axis=0, tiled=True)  78.8 us
    all_gather x1, waiting for transfers between devices, body(): lax.all_gather(own[5][None], 'gx', axis=0, tiled=True)  78.8 us
    dynamic_slice x128, local copies, waits for them, and re-layouts, body(): prefix, _ = lax.scan(take_lower, identity, (indices, table))  75.1 us
    select_n x64, other arithmetic, take_higher(): jnp.where(keep, fresh, older)  67.8 us
  transfers between devices with their start and end apart: 8, of which 7 were waited for; matrix products, arithmetic and copies ran while one was open for 0% of the time, Pallas kernels for 0%

commit v1 on v0

v1 whole, which is shorter than its diff:
```python
import functools

import jax
import jax.numpy as jnp
from jax import lax
from jax.experimental import pallas as pl
from jax.experimental.pallas import tpu as pltpu
from jax.sharding import PartitionSpec as P

MATS = 8
RX = 65536
GROUP = 8
MESH = pl.DeviceIdType.MESH


def look_up(material, table):
    low = (material & 1) == 1
    mid = (material & 2) == 2
    high = material >= 4
    pairs = [jnp.where(low, table[2 * k + 1], table[2 * k]) for k in range(4)]
    quads = [jnp.where(mid, pairs[1], pairs[0]), jnp.where(mid, pairs[3], pairs[2])]
    return jnp.where(high, quads[1], quads[0])


def merge_matrix(left, right):
    ground = left[2] + right[1]
    inverse = 1.0 / (left[0] + right[0] + ground)
    to_left = left[0] * inverse
    to_right = right[0] * inverse
    joined = (to_left * right[0], left[1] + to_left * ground, right[2] + to_right * ground)
    return joined, (inverse, to_left, to_right)


def build_matrix(segments, low, high):
    if high - low == 1:
        return segments[low], None
    mid = (low + high) // 2
    left, left_tree = build_matrix(segments, low, mid)
    right, right_tree = build_matrix(segments, mid, high)
    joined, weights = merge_matrix(left, right)
    return joined, (mid - 1, weights, left_tree, right_tree)


def build_source(tree, sources, low, high, levels):
    if tree is None:
        return sources[low]
    node, (inverse, to_left, to_right), left_tree, right_tree = tree
    left = build_source(left_tree, sources, low, node + 1, levels)
    right = build_source(right_tree, sources, node + 1, high, levels)
    source = left[1] + right[0]
    levels[node] = source * inverse
    return left[0] + to_left * source, right[1] + to_right * source


def spread(tree, levels, before, after, values):
    if tree is None:
        return
    node, (_, to_left, to_right), left_tree, right_tree = tree
    value = levels[node] + to_left * before + to_right * after
    values[node] = value
    spread(left_tree, levels, before, value, values)
    spread(right_tree, levels, value, after, values)


def kernel(groups, columns, table_ref, p_hbm, vy_hbm, vz_hbm, mat_hbm, q_out, vy_out, vz_out,
           p_v, vy_v, vz_v, mat_v, vyn_v, vzn_v, r_v, a_v, tr_v, e_v, q_v,
           edge, edge_mat, halo, halo_mat,
           am_send, am_recv, as_send, as_recv, bm_send, bm_recv, bs_send, bs_recv,
           nodes_b, db_recv, nodes_a, da_recv,
           in_sem, edge_sem, out_sem, halo_send, halo_recv,
           am_ss, am_rs, as_ss, as_rs, bm_ss, bm_rs, bs_ss, bs_rs, db_ss, db_rs, da_ss, da_rs, ring_sem):
    cells, rows_y, lanes = vy_v.shape
    rows_a = rows_y // GROUP
    rows_b = rows_a // groups
    gx = lax.axis_index("gx")
    gy = lax.axis_index("gy")
    z = gx // GROUP
    a = gx % GROUP
    base = z * GROUP
    up = lax.rem(z + 1, groups) * GROUP + a
    down = lax.rem(z + groups - 1, groups) * GROUP + a
    ring = (up,) if groups == 2 else (up, down)
    has_above = gy < columns - 1
    has_below = gy > 0

    loads = [
        pltpu.make_async_copy(mat_hbm, mat_v, in_sem.at[0]),
        pltpu.make_async_copy(p_hbm, p_v.at[:, 0:rows_y, :], in_sem.at[1]),
        pltpu.make_async_copy(vy_hbm, vy_v, in_sem.at[2]),
        pltpu.make_async_copy(vz_hbm, vz_v, in_sem.at[3]),
    ]

    barrier = pltpu.get_barrier_semaphore()
    for k in range(1, GROUP):
        pl.semaphore_signal(barrier, inc=1, device_id=(base + lax.rem(a + k, GROUP), gy), device_id_type=MESH)
    for peer in ring:
        pl.semaphore_signal(barrier, inc=1, device_id=(peer, gy), device_id_type=MESH)

    @pl.when(has_above)
    def _():
        pl.semaphore_signal(barrier, inc=1, device_id=(gx, gy + 1), device_id_type=MESH)

    @pl.when(has_below)
    def _():
        pl.semaphore_signal(barrier, inc=1, device_id=(gx, gy - 1), device_id_type=MESH)

    for copy in loads:
        copy.start()
    last = pl.ds(rows_y - 1, 1)
    first = pl.ds(0, 1)
    edges = [
        pltpu.make_async_copy(mat_hbm.at[:, last, :], edge_mat, edge_sem.at[0]),
        pltpu.make_async_copy(p_hbm.at[:, last, :], edge.at[0], edge_sem.at[1]),
        pltpu.make_async_copy(vy_hbm.at[:, last, :], edge.at[1], edge_sem.at[2]),
        pltpu.make_async_copy(p_hbm.at[:, first, :], edge.at[2], edge_sem.at[3]),
    ]
    for copy in edges:
        copy.start()

    pl.semaphore_wait(barrier, GROUP - 1 + len(ring) + has_above.astype(jnp.int32) + has_below.astype(jnp.int32))

    def halo_up(k, source, target):
        return pltpu.make_async_remote_copy(
            src_ref=source, dst_ref=target, send_sem=halo_send.at[k], recv_sem=halo_recv.at[k],
            device_id=(gx, gy + 1), device_id_type=MESH)

    ups = [
        halo_up(0, mat_hbm.at[:, last, :], halo_mat),
        halo_up(1, p_hbm.at[:, last, :], halo.at[0]),
        halo_up(2, vy_hbm.at[:, last, :], halo.at[1]),
    ]
    goes_down = pltpu.make_async_remote_copy(
        src_ref=p_hbm.at[:, first, :], dst_ref=halo.at[2], send_sem=halo_send.at[3], recv_sem=halo_recv.at[3],
        device_id=(gx, gy - 1), device_id_type=MESH)

    @pl.when(has_above)
    def _():
        for copy in ups:
            copy.start()

    @pl.when(has_below)
    def _():
        goes_down.start()

    stages = groups // 2 - 1
    for stage in range(stages):
        for peer in ring:
            if stage == 0:
                pl.semaphore_signal(ring_sem.at[0], inc=1, device_id=(peer, gy), device_id_type=MESH)

    table = [table_ref[k] for k in range(MATS)]
    scale = 1.0 / RX

    loads[0].wait()
    loads[1].wait()
    loads[2].wait()
    loads[3].wait()
    row_of = lax.broadcasted_iota(jnp.int32, (rows_a, lanes), 0)
    lane_of = lax.broadcasted_iota(jnp.int32, (rows_a, lanes), 1)

    def at_rows(index, offset=0):
        return pl.ds(pl.multiple_of(index * rows_a + offset, 8), rows_a)

    def first_pass(index, matrix_ref):
        here = at_rows(index)
        after = pl.ds(pl.multiple_of(index * rows_a + rows_a, 8), 8)
        conductance = left_ground = carried = None
        for x in range(cells):
            weight = 1.0 + look_up(mat_v[x, here, :], table)
            damping = 1.0 / weight
            excess = weight * scale
            pressure = p_v[x, here, :]
            upper = pltpu.roll(pressure, rows_a - 1, axis=0)
            upper = jnp.where(row_of == rows_a - 1, p_v[x, after, :][0:1, :], upper)
            vyn_v[x, pl.ds(pl.multiple_of(index * rows_a + 8, 8), rows_a), :] = damping * (
                vy_v[x, here, :] - 0.5 * (upper - pressure))
            beyond = jnp.where(lane_of == lanes - 1, 0.0, pltpu.roll(pressure, lanes - 1, axis=1))
            vzn_v[x, here, :] = damping * (vz_v[x, here, :] - 0.5 * (beyond - pressure))
            if x == 0:
                ground = excess
                inverse = 1.0 / (2.0 + ground)
                conductance = inverse
                left_ground = conductance * ground
            elif x < cells - 1:
                ground = excess + carried
                inverse = 1.0 / (conductance + 1.0 + ground)
                conductance = conductance * inverse
                left_ground = left_ground + conductance * ground
            else:
                ground = excess + carried
            if x < cells - 1:
                carried = ground * inverse
                r_v[x, here, :] = inverse
                a_v[x, here, :] = conductance
        matrix_ref[0] = conductance
        matrix_ref[1] = left_ground
        matrix_ref[2] = ground

    def send(source, target, ss, rs, device):
        return pltpu.make_async_remote_copy(
            src_ref=source, dst_ref=target, send_sem=ss, recv_sem=rs, device_id=(device, gy), device_id_type=MESH)

    def matrix_to(k):
        peer = lax.rem(a + k, GROUP)
        return send(am_send.at[peer], am_recv.at[a], am_ss.at[peer], am_rs.at[a], base + peer)

    def source_to(k):
        peer = lax.rem(a + k, GROUP)
        return send(as_send.at[peer], as_recv.at[a], as_ss.at[peer], as_rs.at[a], base + peer)

    p_v[:, pl.ds(rows_y, 8), :] = jnp.zeros((cells, 8, lanes), jnp.float32)

    def first_loop(k, _):
        peer = lax.rem(a + k, GROUP)
        first_pass(peer, am_send.at[peer])
        matrix_to(k).start()
        return 0

    lax.fori_loop(1, GROUP, first_loop, 0)
    first_pass(a, am_recv.at[a])

    pltpu.make_async_copy(vzn_v, vz_out, out_sem.at[0]).start()

    for copy in edges:
        copy.wait()

    @pl.when(has_below)
    def _():
        for copy in ups:
            copy.wait_recv()

    @pl.when(has_above)
    def _():
        goes_down.wait_recv()

    own_damping = 1.0 / (1.0 + look_up(edge_mat[...], table))
    above = jnp.where(has_above, halo[2], 0.0)
    last_row = own_damping * (edge[1] - 0.5 * (above - edge[0]))
    below_damping = 1.0 / (1.0 + look_up(halo_mat[...], table))
    below_row = below_damping * (halo[1] - 0.5 * (edge[2] - halo[0]))
    below_row = jnp.where(has_below, below_row, 0.0)
    vyn_v[:, pl.ds(rows_y + 7, 1), :] = last_row
    vyn_v[:, pl.ds(7, 1), :] = below_row
    pltpu.make_async_copy(vyn_v.at[:, pl.ds(8, rows_y), :], vy_out, out_sem.at[1]).start()

    def second_pass(index, source_ref):
        here = at_rows(index)
        behind = pl.ds(pl.multiple_of(index * rows_a, 8), 8)
        total = left_source = None
        for x in range(cells):
            vyn = vyn_v[x, pl.ds(pl.multiple_of(index * rows_a + 8, 8), rows_a), :]
            lower = pltpu.roll(vyn, 1, axis=0)
            lower = jnp.where(row_of == 0, vyn_v[x, behind, :][7:8, :], lower)
            vzn = vzn_v[x, here, :]
            before = jnp.where(lane_of == 0, 0.0, pltpu.roll(vzn, 1, axis=1))
            source = (p_v[x, here, :] - 0.5 * (vyn - lower + vzn - before)) * scale
            total = source if x == 0 else source + passed
            if x < cells - 1:
                passed = total * r_v[x, here, :]
                tr_v[x, here, :] = passed
                share = total * a_v[x, here, :]
                left_source = share if x == 0 else left_source + share
        source_ref[0] = left_source
        source_ref[1] = total

    def second_loop(k, _):
        peer = lax.rem(a + k, GROUP)
        second_pass(peer, as_send.at[peer])
        source_to(k).start()
        return 0

    lax.fori_loop(1, GROUP, second_loop, 0)
    second_pass(a, as_recv.at[a])

    for stage in range(stages):
        pl.semaphore_wait(ring_sem.at[stage], len(ring))
        if stage + 1 < stages:
            for peer in ring:
                pl.semaphore_signal(ring_sem.at[stage + 1], inc=1, device_id=(peer, gy), device_id_type=MESH)

    def wait_a(k, _):
        peer = lax.rem(a + k, GROUP)
        send(am_send.at[peer], am_recv.at[peer], am_ss.at[peer], am_rs.at[peer], base + peer).wait()
        return 0

    lax.fori_loop(1, GROUP, wait_a, 0)
    segment, tree = build_matrix([tuple(am_recv[k, v] for v in range(3)) for k in range(GROUP)], 0, GROUP)
    for k in range(groups):
        for v in range(3):
            bm_send[k, v] = segment[v][rows_b * k:rows_b * (k + 1), :]
    bm_recv[z] = bm_send[z]

    def to_ring(k, source, target, ss, rs):
        peer = lax.rem(z + k, groups)
        return send(source.at[peer], target.at[z], ss.at[peer], rs.at[z], peer * GROUP + a)

    def from_ring(k, source, target, ss, rs):
        peer = lax.rem(z + k, groups)
        return send(source.at[peer], target.at[peer], ss.at[peer], rs.at[peer], peer * GROUP + a)

    for k in range(1, groups):
        to_ring(k, bm_send, bm_recv, bm_ss, bm_rs).start()

    def wait_as(k, _):
        peer = lax.rem(a + k, GROUP)
        send(as_send.at[peer], as_recv.at[peer], as_ss.at[peer], as_rs.at[peer], base + peer).wait()
        return 0

    lax.fori_loop(1, GROUP, wait_as, 0)
    levels = [None] * GROUP
    pair = build_source(tree, [(as_recv[k, 0], as_recv[k, 1]) for k in range(GROUP)], 0, GROUP, levels)
    for k in range(groups):
        for v in range(2):
            bs_send[k, v] = pair[v][rows_b * k:rows_b * (k + 1), :]
    bs_recv[z] = bs_send[z]
    for k in range(1, groups):
        to_ring(k, bs_send, bs_recv, bs_ss, bs_rs).start()

    for k in range(1, groups):
        from_ring(k, bm_send, bm_recv, bm_ss, bm_rs).wait()
    whole, tree_b = build_matrix([tuple(bm_recv[k, v] for v in range(3)) for k in range(groups)], 0, groups)
    end_inverse = 1.0 / (whole[0] + (whole[2] + 1.0))
    for k in range(1, groups):
        from_ring(k, bs_send, bs_recv, bs_ss, bs_rs).wait()
    levels_b = [None] * groups
    sums = build_source(tree_b, [(bs_recv[k, 0], bs_recv[k, 1]) for k in range(groups)], 0, groups, levels_b)
    values_b = [None] * groups
    nothing = jnp.zeros((rows_b, lanes), jnp.float32)
    values_b[groups - 1] = sums[1] * end_inverse
    spread(tree_b, levels_b, nothing, values_b[groups - 1], values_b)
    nodes_b[0] = nothing
    for k in range(groups):
        nodes_b[k + 1] = values_b[k]

    def back_b(k, slot):
        peer = lax.rem(z + k, groups)
        return send(nodes_b.at[pl.ds(peer, 2)], db_recv.at[slot(peer)], db_ss.at[peer], db_rs.at[slot(peer)],
                    peer * GROUP + a)

    for k in range(1, groups):
        back_b(k, lambda peer: z).start()
    db_recv[z] = nodes_b[pl.ds(z, 2)]
    for k in range(1, groups):
        back_b(k, lambda peer: peer).wait()
    before_all = jnp.concatenate([db_recv[k, 0] for k in range(groups)], axis=0)
    after_all = jnp.concatenate([db_recv[k, 1] for k in range(groups)], axis=0)
    values = [None] * GROUP
    values[GROUP - 1] = after_all
    spread(tree, levels, before_all, after_all, values)
    nodes_a[0] = before_all
    for k in range(GROUP):
        nodes_a[k + 1] = values[k]

    def back_a(k, owner):
        peer = lax.rem(a + k, GROUP)
        slot = owner(peer)
        return send(nodes_a.at[pl.ds(peer, 2)], da_recv.at[slot], da_ss.at[peer], da_rs.at[slot], base + peer)

    def back_loop(k, _):
        back_a(k, lambda peer: a).start()
        return 0

    lax.fori_loop(1, GROUP, back_loop, 0)

    def finish(index, before, after):
        here = at_rows(index)
        q_v[cells - 1, here, :] = after
        for x in range(cells - 2, -1, -1):
            after = tr_v[x, here, :] + r_v[x, here, :] * after + a_v[x, here, :] * before
            q_v[x, here, :] = after
        pltpu.make_async_copy(q_v.at[:, here, :], q_out.at[:, here, :], out_sem.at[2 + index]).start()

    finish(a, nodes_a[a], nodes_a[a + 1])

    def finish_loop(k, _):
        peer = lax.rem(a + GROUP - k, GROUP)
        send(nodes_a.at[pl.ds(peer, 2)], da_recv.at[peer], da_ss.at[peer], da_rs.at[peer], base + peer).wait()
        finish(peer, da_recv[peer, 0], da_recv[peer, 1])
        return 0

    lax.fori_loop(1, GROUP, finish_loop, 0)

    @pl.when(has_above)
    def _():
        for copy in ups:
            copy.wait_send()

    @pl.when(has_below)
    def _():
        goes_down.wait_send()

    pltpu.make_async_copy(vzn_v, vz_out, out_sem.at[0]).wait()
    pltpu.make_async_copy(vyn_v.at[:, pl.ds(8, rows_y), :], vy_out, out_sem.at[1]).wait()

    def drain(k, _):
        here = at_rows(k)
        pltpu.make_async_copy(q_v.at[:, here, :], q_out.at[:, here, :], out_sem.at[2 + k]).wait()
        return 0

    lax.fori_loop(0, GROUP, drain, 0)


def solution(mesh):
    groups = mesh.shape["gx"] // GROUP
    columns = mesh.shape["gy"]

    def body(pressure, vel_y, vel_z, material, absorb_table):
        cells, rows_y, lanes = pressure.shape
        rows_a = rows_y // GROUP
        rows_b = rows_a // groups
        f32 = jnp.float32
        vmem = pltpu.VMEM
        dma = pltpu.SemaphoreType.DMA
        scratch = [
            vmem((cells, rows_y + 8, lanes), f32),
            vmem((cells, rows_y, lanes), f32),
            vmem((cells, rows_y, lanes), f32),
            vmem((cells, rows_y, lanes), jnp.int32),
            vmem((cells, rows_y + 8, lanes), f32),
            vmem((cells, rows_y, lanes), f32),
            vmem((cells - 1, rows_y, lanes), f32),
            vmem((cells - 1, rows_y, lanes), f32),
            vmem((cells - 1, rows_y, lanes), f32),
            vmem((8, lanes), f32),
            vmem((cells, rows_y, lanes), f32),
            vmem((3, cells, 1, lanes), f32),
            vmem((cells, 1, lanes), jnp.int32),
            vmem((3, cells, 1, lanes), f32),
            vmem((cells, 1, lanes), jnp.int32),
            vmem((GROUP, 3, rows_a, lanes), f32),
            vmem((GROUP, 3, rows_a, lanes), f32),
            vmem((GROUP, 2, rows_a, lanes), f32),
            vmem((GROUP, 2, rows_a, lanes), f32),
            vmem((groups, 3, rows_b, lanes), f32),
            vmem((groups, 3, rows_b, lanes), f32),
            vmem((groups, 2, rows_b, lanes), f32),
            vmem((groups, 2, rows_b, lanes), f32),
            vmem((groups + 1, rows_b, lanes), f32),
            vmem((groups, 2, rows_b, lanes), f32),
            vmem((GROUP + 1, rows_a, lanes), f32),
            vmem((GROUP, 2, rows_a, lanes), f32),
            dma((4,)), dma((4,)), dma((2 + GROUP,)), dma((4,)), dma((4,)),
            dma((GROUP,)), dma((GROUP,)), dma((GROUP,)), dma((GROUP,)),
            dma((groups,)), dma((groups,)), dma((groups,)), dma((groups,)),
            dma((groups,)), dma((groups,)), dma((GROUP,)), dma((GROUP,)),
            pltpu.SemaphoreType.REGULAR((max(1, groups // 2 - 1),)),
        ]
        anywhere = pl.BlockSpec(memory_space=pltpu.HBM)
        return pl.pallas_call(
            functools.partial(kernel, groups, columns),
            out_shape=[jax.ShapeDtypeStruct(pressure.shape, f32)] * 3,
            in_specs=[pl.BlockSpec(memory_space=pltpu.SMEM)] + [anywhere] * 4,
            out_specs=[anywhere] * 3,
            scratch_shapes=scratch,
            compiler_params=pltpu.CompilerParams(collective_id=0, has_side_effects=True, vmem_limit_bytes=40 * 1024 * 1024),
            name="acoustic_step",
        )(absorb_table, pressure, vel_y, vel_z, material)

    return jax.shard_map(
        body,
        mesh=mesh,
        in_specs=(P("gx", "gy", None), P("gx", "gy", None), P("gx", "gy", None), P("gx", "gy", None), P()),
        out_specs=(P("gx", "gy", None), P("gx", "gy", None), P("gx", "gy", None)),
        check_vma=False,
    )
```

time: 859 us -> 38.8 us (0.05); the launches traced: 849 us -> 38.5 us
  waiting for transfers between devices: 480 us -> 0 us
  other arithmetic: 172 us -> 0 us
  loops' own time: 86.8 us -> 0 us
  local copies, waits for them, and re-layouts: 89.3 us -> 7.19 us
  Pallas kernels: 0 us -> 30.7 us
  between operations: 14.4 us -> 0.65 us
    all_gather x6 -> x0, waiting for transfers between devices: 476 us -> none  [the longest x1 81.3 us: body(): lax.all_gather(own[3][None], 'gx', axis=0, tiled=True)]
    select_n x130 -> x0, other arithmetic: 135 us -> none  [the longest x64 67.8 us: take_higher(): jnp.where(keep, fresh, older)]
    another operation x4 -> x0, loops' own time: 86.8 us -> none  [the longest x1 43.3 us: body(): suffix, _ = lax.scan(take_higher, identity, (indices, table), reverse=True)]
    dynamic_slice x128 -> x0, local copies, waits for them, and re-layouts: 75.1 us -> none  [body(): prefix, _ = lax.scan(take_lower, identity, (indices, table))]
    pallas_call x0 -> x1, Pallas kernels: none -> 30.7 us  [body(): pl.pallas_call(functools.partial(kernel, groups, columns), out_shape=[jax...]
    dynamic_update_slice x24 -> x0, other arithmetic: 21.4 us -> none  [sweep_lines(): _, (inverses, values) = lax.scan(forward, start, (excess, stacked))]
    mul x9 -> x0, other arithmetic: 13.4 us -> none  [the longest x8 6.98 us: forward(): carried_next = (excess_row + carried) * inverse]
  transfers between devices with their start and end apart: 8 -> 0, of which waited for: 7 -> 0; matrix products, arithmetic and copies ran while one was open for 0% -> 0% of each run, Pallas kernels for 0% -> 0%
where the time goes in v1:
time: 38.8 us; the launch traced here: 38.5 us
  Pallas kernels  30.7 us (79%)
  local copies, waits for them, and re-layouts  7.19 us (19%)
  between operations  0.65 us (2%)
    pallas_call x1, Pallas kernels, body(): pl.pallas_call(functools.partial(kernel, groups, columns), out_shape=[jax...  30.7 us
    unnamed x13, local copies, waits for them, and re-layouts  7.19 us

profile of v1, /device:TPU:1, one launch (start us, length us, event | category | flops | bytes accessed | tf_op | source)
XLA Modules:
  0.0 38.5 jit_solution(7464864151946200374)
XLA Ops:
  0.6 0.0 copy-start
  0.6 1.0 %copy-done = f32[8,128,128]{2,1,0:T(8,128)S(1)} copy-done((f32[8,128,128]{2,1,0:T(8,128)S(1)}, f32[8,128,128]{2,1,0:T(8,128)}, u32[]{:S(2)}) %copy-start) | copy-done | bytes 524312
  1.7 0.0 copy-start.1
  1.7 1.0 %copy-done.1 = f32[8,128,128]{2,1,0:T(8,128)S(1)} copy-done((f32[8,128,128]{2,1,0:T(8,128)S(1)}, f32[8,128,128]{2,1,0:T(8,128)}, u32[]{:S(2)}) %copy-start.1) | copy-done | bytes 524312
  2.7 0.0 copy-start.2
  2.7 1.0 %copy-done.2 = f32[8,128,128]{2,1,0:T(8,128)S(1)} copy-done((f32[8,128,128]{2,1,0:T(8,128)S(1)}, f32[8,128,128]{2,1,0:T(8,128)}, u32[]{:S(2)}) %copy-start.2) | copy-done | bytes 524312
  3.8 0.0 copy-start.3
  3.8 1.0 %copy-done.3 = s32[8,128,128]{2,1,0:T(8,128)S(1)} copy-done((s32[8,128,128]{2,1,0:T(8,128)S(1)}, s32[8,128,128]{2,1,0:T(8,128)}, u32[]{:S(2)}) %copy-start.3) | copy-done | bytes 524312
  4.8 0.0 copy-start.4
  4.8 0.7 %copy-done.4 = f32[8]{0:T(128)S(1)} copy-done((f32[8]{0:T(128)S(1)}, f32[8]{0:T(128)}, u32[]{:S(2)}) %copy-start.4) | copy-done | bytes 56
  5.5 30.7 %acoustic_step.1 = (f32[8,128,128]{2,1,0:T(8,128)S(1)}, f32[8,128,128]{2,1,0:T(8,128)S(1)}, f32[8,128,128]{2,1,0:T(8,128)S(1)}) custom-call(f32[8]{0:T(128)S(1)} %copy-done.4, f32[8,128,128]{2,1,0:T(8,128)S(1)} %copy-done, f32[8,128,128]{2,1,0:T(8,128)S(1)} %copy-done.1, f32[8,128,128]{2,1,0:T(8,128)S(1)} %copy-done.2, s32[8,128,128]{2,1,0:T(8,128)S(1)} %copy-done.3), custom_call_target="tpu_custom_call" | custom-call | tf_op jit(solution)/shard_map/acoustic_step/pallas_call | solution.py:449
  36.2 0.8 %copy.11 = f32[8,128,128]{2,1,0:T(8,128)} copy(f32[8,128,128]{2,1,0:T(8,128)S(1)} %get-tuple-element.6) | data formatting | bytes 1048576
  37.0 0.8 %copy.12 = f32[8,128,128]{2,1,0:T(8,128)} copy(f32[8,128,128]{2,1,0:T(8,128)S(1)} %get-tuple-element.7) | data formatting | bytes 1048576
  37.8 0.8 %copy.13 = f32[8,128,128]{2,1,0:T(8,128)} copy(f32[8,128,128]{2,1,0:T(8,128)S(1)} %get-tuple-element.8) | data formatting | bytes 1048576
Async XLA Ops:
  0.6 1.0 %copy-start = (f32[8,128,128]{2,1,0:T(8,128)S(1)}, f32[8,128,128]{2,1,0:T(8,128)}, u32[]{:S(2)}) copy-start(f32[8,128,128]{2,1,0:T(8,128)} %p_hbm.1) | copy-start | bytes 1572868
  1.7 1.0 %copy-start.1 = (f32[8,128,128]{2,1,0:T(8,128)S(1)}, f32[8,128,128]{2,1,0:T(8,128)}, u32[]{:S(2)}) copy-start(f32[8,128,128]{2,1,0:T(8,128)} %vy_hbm.1) | copy-start | bytes 1572868
  2.7 1.0 %copy-start.2 = (f32[8,128,128]{2,1,0:T(8,128)S(1)}, f32[8,128,128]{2,1,0:T(8,128)}, u32[]{:S(2)}) copy-start(f32[8,128,128]{2,1,0:T(8,128)} %vz_hbm.1) | copy-start | bytes 1572868
  3.8 1.0 %copy-start.3 = (s32[8,128,128]{2,1,0:T(8,128)S(1)}, s32[8,128,128]{2,1,0:T(8,128)}, u32[]{:S(2)}) copy-start(s32[8,128,128]{2,1,0:T(8,128)} %mat_hbm.1) | copy-start | bytes 1572868
  4.8 0.7 %copy-start.4 = (f32[8]{0:T(128)S(1)}, f32[8]{0:T(128)}, u32[]{:S(2)}) copy-start(f32[8]{0:T(128)} %table_ref.1) | copy-start | bytes 100

commit v2 on v1

--- a/solution.py
+++ b/solution.py
@@ -11,6 +11,8 @@
 RX = 65536
 GROUP = 8
 MESH = pl.DeviceIdType.MESH
+LIMIT1 = 60 * 1024 * 1024
+LIMIT2 = 8 * 1024 * 1024
 
 
 def look_up(material, table):
@@ -62,12 +64,13 @@
     spread(right_tree, levels, value, after, values)
 
 
-def kernel(groups, columns, table_ref, p_hbm, vy_hbm, vz_hbm, mat_hbm, q_out, vy_out, vz_out,
-           p_v, vy_v, vz_v, mat_v, vyn_v, vzn_v, r_v, a_v, tr_v, e_v, q_v,
+def kernel(groups, columns, table_ref, p_hbm, vy_hbm, vz_hbm, mat_hbm,
+           vyn_v, vzn_v, r_v, a_v, tr_v, ends_v,
+           p_v, vy_v, vz_v, mat_v,
            edge, edge_mat, halo, halo_mat,
            am_send, am_recv, as_send, as_recv, bm_send, bm_recv, bs_send, bs_recv,
            nodes_b, db_recv, nodes_a, da_recv,
-           in_sem, edge_sem, out_sem, halo_send, halo_recv,
+           in_sem, edge_sem, halo_send, halo_recv,
            am_ss, am_rs, as_ss, as_rs, bm_ss, bm_rs, bs_ss, bs_rs, db_ss, db_rs, da_ss, da_rs, ring_sem):
     cells, rows_y, lanes = vy_v.shape
     rows_a = rows_y // GROUP
@@ -219,8 +222,6 @@
     lax.fori_loop(1, GROUP, first_loop, 0)
     first_pass(a, am_recv.at[a])
 
-    pltpu.make_async_copy(vzn_v, vz_out, out_sem.at[0]).start()
-
     for copy in edges:
         copy.wait()
 
@@ -241,7 +242,6 @@
     below_row = jnp.where(has_below, below_row, 0.0)
     vyn_v[:, pl.ds(rows_y + 7, 1), :] = last_row
     vyn_v[:, pl.ds(7, 1), :] = below_row
-    pltpu.make_async_copy(vyn_v.at[:, pl.ds(8, rows_y), :], vy_out, out_sem.at[1]).start()
 
     def second_pass(index, source_ref):
         here = at_rows(index)
@@ -362,42 +362,49 @@
 
     lax.fori_loop(1, GROUP, back_loop, 0)
 
-    def finish(index, before, after):
-        here = at_rows(index)
+    ends_v[a, 0] = nodes_a[a]
+    ends_v[a, 1] = nodes_a[a + 1]
+
+    def back_wait(k, _):
+        peer = lax.rem(a + GROUP - k, GROUP)
+        send(nodes_a.at[pl.ds(peer, 2)], da_recv.at[peer], da_ss.at[peer], da_rs.at[peer], base + peer).wait()
+        ends_v[peer] = da_recv[peer]
+        return 0
+
+    lax.fori_loop(1, GROUP, back_wait, 0)
+
+    @pl.when(has_above)
+    def _():
+        for copy in ups:
+            copy.wait_send()
+
+    @pl.when(has_below)
+    def _():
+        goes_down.wait_send()
+
+
+def finish(vyn_v, vzn_v, r_v, a_v, tr_v, ends_v, q_out, vy_out, vz_out, q_v, out_sem):
+    cells, rows_y, _ = vzn_v.shape
+    rows_a = rows_y // GROUP
+    velocities = [
+        pltpu.make_async_copy(vzn_v, vz_out, out_sem.at[0]),
+        pltpu.make_async_copy(vyn_v.at[:, pl.ds(8, rows_y), :], vy_out, out_sem.at[1]),
+    ]
+    pressures = []
+    for index in range(GROUP):
+        here = pl.ds(index * rows_a, rows_a)
+        before, after = ends_v[index, 0], ends_v[index, 1]
         q_v[cells - 1, here, :] = after
         for x in range(cells - 2, -1, -1):
             after = tr_v[x, here, :] + r_v[x, here, :] * after + a_v[x, here, :] * before
             q_v[x, here, :] = after
-        pltpu.make_async_copy(q_v.at[:, here, :], q_out.at[:, here, :], out_sem.at[2 + index]).start()
-
-    finish(a, nodes_a[a], nodes_a[a + 1])
-
-    def finish_loop(k, _):
-        peer = lax.rem(a + GROUP - k, GROUP)
-        send(nodes_a.at[pl.ds(peer, 2)], da_recv.at[peer], da_ss.at[peer], da_rs.at[peer], base + peer).wait()
-        finish(peer, da_recv[peer, 0], da_recv[peer, 1])
-        return 0
-
-    lax.fori_loop(1, GROUP, finish_loop, 0)
-
-    @pl.when(has_above)
-    def _():
-        for copy in ups:
-            copy.wait_send()
-
-    @pl.when(has_below)
-    def _():
-        goes_down.wait_send()
-
-    pltpu.make_async_copy(vzn_v, vz_out, out_sem.at[0]).wait()
-    pltpu.make_async_copy(vyn_v.at[:, pl.ds(8, rows_y), :], vy_out, out_sem.at[1]).wait()
-
-    def drain(k, _):
-        here = at_rows(k)
-        pltpu.make_async_copy(q_v.at[:, here, :], q_out.at[:, here, :], out_sem.at[2 + k]).wait()
-        return 0
-
-    lax.fori_loop(0, GROUP, drain, 0)
+        pressures.append(pltpu.make_async_copy(q_v.at[:, here, :], q_out.at[:, here, :], out_sem.at[2 + index]))
+        pressures[-1].start()
+        if index == 0:
+            for copy in velocities:
+                copy.start()
+    for copy in velocities + pressures:
+        copy.wait()
 
 
 def solution(mesh):
@@ -411,18 +418,19 @@
         f32 = jnp.float32
         vmem = pltpu.VMEM
         dma = pltpu.SemaphoreType.DMA
+        kept = [
+            vmem((cells, rows_y + 8, lanes), f32),
+            vmem((cells, rows_y, lanes), f32),
+            vmem((cells - 1, rows_y, lanes), f32),
+            vmem((cells - 1, rows_y, lanes), f32),
+            vmem((cells - 1, rows_y, lanes), f32),
+            vmem((GROUP, 2, rows_a, lanes), f32),
+        ]
         scratch = [
             vmem((cells, rows_y + 8, lanes), f32),
             vmem((cells, rows_y, lanes), f32),
             vmem((cells, rows_y, lanes), f32),
             vmem((cells, rows_y, lanes), jnp.int32),
-            vmem((cells, rows_y + 8, lanes), f32),
-            vmem((cells, rows_y, lanes), f32),
-            vmem((cells - 1, rows_y, lanes), f32),
-            vmem((cells - 1, rows_y, lanes), f32),
-            vmem((cells - 1, rows_y, lanes), f32),
-            vmem((8, lanes), f32),
-            vmem((cells, rows_y, lanes), f32),
             vmem((3, cells, 1, lanes), f32),
             vmem((cells, 1, lanes), jnp.int32),
             vmem((3, cells, 1, lanes), f32),
@@ -439,22 +447,32 @@
             vmem((groups, 2, rows_b, lanes), f32),
             vmem((GROUP + 1, rows_a, lanes), f32),
             vmem((GROUP, 2, rows_a, lanes), f32),
-            dma((4,)), dma((4,)), dma((2 + GROUP,)), dma((4,)), dma((4,)),
+            dma((4,)), dma((4,)), dma((4,)), dma((4,)),
             dma((GROUP,)), dma((GROUP,)), dma((GROUP,)), dma((GROUP,)),
             dma((groups,)), dma((groups,)), dma((groups,)), dma((groups,)),
             dma((groups,)), dma((groups,)), dma((GROUP,)), dma((GROUP,)),
             pltpu.SemaphoreType.REGULAR((max(1, groups // 2 - 1),)),
         ]
-        anywhere = pl.BlockSpec(memory_space=pltpu.HBM)
+        hbm = pl.BlockSpec(memory_space=pltpu.HBM)
+        local = pl.BlockSpec(memory_space=pltpu.VMEM)
+        held = pl.pallas_call(
+            functools.partial(kernel, groups, columns),
+            out_shape=kept,
+            in_specs=[pl.BlockSpec(memory_space=pltpu.SMEM)] + [hbm] * 4,
+            out_specs=[local] * len(kept),
+            scratch_shapes=scratch,
+            compiler_params=pltpu.CompilerParams(collective_id=0, has_side_effects=True, vmem_limit_bytes=LIMIT1),
+            name="exchange",
+        )(absorb_table, pressure, vel_y, vel_z, material)
         return pl.pallas_call(
-            functools.partial(kernel, groups, columns),
+            finish,
             out_shape=[jax.ShapeDtypeStruct(pressure.shape, f32)] * 3,
-            in_specs=[pl.BlockSpec(memory_space=pltpu.SMEM)] + [anywhere] * 4,
-            out_specs=[anywhere] * 3,
-            scratch_shapes=scratch,
-            compiler_params=pltpu.CompilerParams(collective_id=0, has_side_effects=True, vmem_limit_bytes=40 * 1024 * 1024),
-            name="acoustic_step",
-        )(absorb_table, pressure, vel_y, vel_z, material)
+            in_specs=[local] * len(kept),
+            out_specs=[hbm] * 3,
+            scratch_shapes=[vmem((cells, rows_y, lanes), f32), dma((2 + GROUP,))],
+            compiler_params=pltpu.CompilerParams(vmem_limit_bytes=LIMIT2),
+            name="finish",
+        )(*held)
 
     return jax.shard_map(
         body,

time: 38.8 us -> 32.9 us (0.85)
  local copies, waits for them, and re-layouts: 7.19 us -> 0 us
  Pallas kernels: 30.7 us -> 32.1 us
    unnamed x13 -> x0, local copies, waits for them, and re-layouts: 7.19 us -> none
    pallas_call x1 -> x2, Pallas kernels: 30.7 us -> 32.1 us  [the longest x1 30.9 us: body(): pl.pallas_call(functools.partial(kernel, groups, columns), out_shape=kept...]
where the time goes in v2:
time: 32.9 us; the launch traced here: 32.7 us
  Pallas kernels  32.1 us (98%)
  between operations  0.64 us (2%)
    pallas_call x1, Pallas kernels, body(): pl.pallas_call(functools.partial(kernel, groups, columns), out_shape=kept...  30.9 us
    pallas_call x1, Pallas kernels, body(): pl.pallas_call(finish, out_shape=[jax.ShapeDtypeStruct(pressure.shape, f3...  1.24 us

profile of v2, /device:TPU:1, one launch (start us, length us, event | category | flops | bytes accessed | tf_op | source)
XLA Modules:
  0.0 32.7 jit_solution(957800411034902893)
XLA Ops:
  0.6 30.9 %exchange.1 = (f32[8,136,128]{2,1,0:T(8,128)S(1)}, f32[8,128,128]{2,1,0:T(8,128)S(1)}, f32[7,128,128]{2,1,0:T(8,128)S(1)}, f32[7,128,128]{2,1,0:T(8,128)S(1)}, f...) custom-call(f32[8]{0:T(128)} %table_ref.1, f32[8,128,128]{2,1,0:T(8,128)} %p_hbm.1, f32[8,128,128]{2,1,0:T(8,128)} %vy_hbm.1, ...), custom_call_target="tpu_custom_call" | custom-call | tf_op jit(solution)/shard_map/exchange/pallas_call | solution.py:458
  31.5 1.2 %finish.1 = (f32[8,128,128]{2,1,0:T(8,128)}, f32[8,128,128]{2,1,0:T(8,128)}, f32[8,128,128]{2,1,0:T(8,128)}) custom-call(f32[8,136,128]{2,1,0:T(8,128)S(1)} %get-tuple-element.9.vyn_v, f32[8,128,128]{2,1,0:T(8,128)S(1)} %get-tuple-element.10.vzn_v, f32[7,128,128]{2,1,0:T(8,128)S(1)} %get-tuple-element.11.r_v, f32[7,128,128]{2,1,0:T(8,128)S(1)} %get-tuple-element.12.a_v, ...), custom_call_target="tpu_custom_call" | custom-call | tf_op jit(solution)/shard_map/finish/pallas_call | solution.py:467

commit v3 on v2

v3 whole, which is shorter than its diff:
```python
import functools

import jax
import jax.numpy as jnp
from jax import lax
from jax.experimental import pallas as pl
from jax.experimental.pallas import tpu as pltpu
from jax.sharding import PartitionSpec as P

MATS = 8
RX = 65536
GROUP = 8
LIMIT1 = 60 * 1024 * 1024
LIMIT2 = 8 * 1024 * 1024
MESH = pl.DeviceIdType.MESH


def look_up(material, table):
    low = (material & 1) == 1
    mid = (material & 2) == 2
    high = material >= 4
    pairs = [jnp.where(low, table[2 * k + 1], table[2 * k]) for k in range(4)]
    quads = [jnp.where(mid, pairs[1], pairs[0]), jnp.where(mid, pairs[3], pairs[2])]
    return jnp.where(high, quads[1], quads[0])


def merge_matrix(left, right):
    ground = left[2] + right[1]
    inverse = 1.0 / (left[0] + right[0] + ground)
    to_left = left[0] * inverse
    to_right = right[0] * inverse
    joined = (to_left * right[0], left[1] + to_left * ground, right[2] + to_right * ground)
    return joined, (inverse, to_left, to_right)


def build_matrix(segments, low, high):
    if high - low == 1:
        return segments[low], None
    mid = (low + high) // 2
    left, left_tree = build_matrix(segments, low, mid)
    right, right_tree = build_matrix(segments, mid, high)
    joined, weights = merge_matrix(left, right)
    return joined, (mid - 1, weights, left_tree, right_tree)


def build_source(tree, sources, low, high, levels):
    if tree is None:
        return sources[low]
    node, (inverse, to_left, to_right), left_tree, right_tree = tree
    left = build_source(left_tree, sources, low, node + 1, levels)
    right = build_source(right_tree, sources, node + 1, high, levels)
    source = left[1] + right[0]
    levels[node] = source * inverse
    return left[0] + to_left * source, right[1] + to_right * source


def spread(tree, levels, before, after, values):
    if tree is None:
        return
    node, (_, to_left, to_right), left_tree, right_tree = tree
    value = levels[node] + to_left * before + to_right * after
    values[node] = value
    spread(left_tree, levels, before, value, values)
    spread(right_tree, levels, value, after, values)


def kernel(groups, columns, table_hbm, p_hbm, vy_hbm, vz_hbm, mat_hbm,
           vyn_v, vzn_v, q_v,
           table_ref, p_v, vy_v, vz_v, mat_v, d_v, r_v, a_v, tr_v,
           edge, edge_mat, halo, halo_mat,
           am_send, am_recv, as_send, as_recv, bm_send, bm_recv, bs_send, bs_recv,
           nodes_b, db_recv, nodes_a, da_recv,
           table_sem, in_sem, edge_sem, halo_send, halo_recv,
           am_ss, am_rs, as_ss, as_rs, bm_ss, bm_rs, bs_ss, bs_rs, db_ss, db_rs, da_ss, da_rs, x_token, z_token):
    cells, rows_y, lanes = vy_v.shape
    rows_a = rows_y // GROUP
    rows_b = rows_a // 2
    chips = GROUP // 2
    solver = groups - 2
    gx = lax.axis_index("gx")
    gy = lax.axis_index("gy")
    z = gx // GROUP
    a = gx % GROUP
    chip = a // 2
    core = a % 2
    base = z * GROUP
    has_above = gy < columns - 1
    has_below = gy > 0

    def member(dx, dc):
        return lax.rem(chip + dx, chips) * 2 + lax.rem(core + dc, 2)

    def at_z(step):
        return lax.rem(z + step + groups, groups) * GROUP + a

    def signal(semaphore, device_x, device_y=None):
        pl.semaphore_signal(semaphore, inc=1, device_id=(device_x, gy if device_y is None else device_y), device_id_type=MESH)

    table_copy = pltpu.make_async_copy(table_hbm, table_ref, table_sem)
    table_copy.start()

    barrier = pltpu.get_barrier_semaphore()
    beside = [] if chips == 1 else ([1] if chips == 2 else [1, chips - 1])
    ring = [1] if groups == 2 else [1, -1]

    @pl.when(has_above)
    def _():
        signal(barrier, gx, gy + 1)

    @pl.when(has_below)
    def _():
        signal(barrier, gx, gy - 1)

    for dx in beside:
        for dc in range(2):
            signal(barrier, base + member(dx, dc))
    signal(barrier, base + member(0, 1))
    for step in ring:
        signal(barrier, at_z(step))

    loads = [
        pltpu.make_async_copy(mat_hbm, mat_v, in_sem.at[0]),
        pltpu.make_async_copy(p_hbm, p_v.at[:, 0:rows_y, :], in_sem.at[1]),
        pltpu.make_async_copy(vy_hbm, vy_v, in_sem.at[2]),
        pltpu.make_async_copy(vz_hbm, vz_v, in_sem.at[3]),
    ]
    for copy in loads:
        copy.start()
    last = pl.ds(rows_y - 1, 1)
    first = pl.ds(0, 1)
    edges = [
        pltpu.make_async_copy(mat_hbm.at[:, last, :], edge_mat, edge_sem.at[0]),
        pltpu.make_async_copy(p_hbm.at[:, last, :], edge.at[0], edge_sem.at[1]),
        pltpu.make_async_copy(vy_hbm.at[:, last, :], edge.at[1], edge_sem.at[2]),
        pltpu.make_async_copy(p_hbm.at[:, first, :], edge.at[2], edge_sem.at[3]),
    ]
    for copy in edges:
        copy.start()
    p_v[:, pl.ds(rows_y, 8), :] = jnp.zeros((cells, 8, lanes), jnp.float32)

    near = 2 * len(beside) + 1 + len(ring)
    pl.semaphore_wait(barrier, near + has_above.astype(jnp.int32) + has_below.astype(jnp.int32))

    def halo_up(k, source, target):
        return pltpu.make_async_remote_copy(
            src_ref=source, dst_ref=target, send_sem=halo_send.at[k], recv_sem=halo_recv.at[k],
            device_id=(gx, gy + 1), device_id_type=MESH)

    ups = [
        halo_up(0, mat_hbm.at[:, last, :], halo_mat),
        halo_up(1, p_hbm.at[:, last, :], halo.at[0]),
        halo_up(2, vy_hbm.at[:, last, :], halo.at[1]),
    ]
    goes_down = pltpu.make_async_remote_copy(
        src_ref=p_hbm.at[:, first, :], dst_ref=halo.at[2], send_sem=halo_send.at[3], recv_sem=halo_recv.at[3],
        device_id=(gx, gy - 1), device_id_type=MESH)

    @pl.when(has_above)
    def _():
        for copy in ups:
            copy.start()

    @pl.when(has_below)
    def _():
        goes_down.start()

    if chips > 2:
        signal(x_token, base + member(chips - 1, 0))

    half = groups // 2
    if groups > 2:
        @pl.when(z == groups - 1)
        def _():
            signal(z_token, at_z(1))

        if solver > half:
            @pl.when(z == solver)
            def _():
                signal(z_token, at_z(-1))

    scale = 1.0 / RX
    row_of = lax.broadcasted_iota(jnp.int32, (rows_a, lanes), 0)
    lane_of = lax.broadcasted_iota(jnp.int32, (rows_a, lanes), 1)

    def at_rows(index, offset=0):
        return pl.ds(pl.multiple_of(index * rows_a + offset, 8), rows_a)

    def send(source, target, ss, rs, device):
        return pltpu.make_async_remote_copy(
            src_ref=source, dst_ref=target, send_sem=ss, recv_sem=rs, device_id=(device, gy), device_id_type=MESH)

    def for_far(visit):
        if chips > 2:
            def far(k, _):
                visit(member(2, k))
                return 0
            lax.fori_loop(0, 2, far, 0)

    def for_close(visit):
        if chips > 2:
            def close(k, _):
                visit(member(1 + 2 * (k % 2), k // 2))
                return 0
            lax.fori_loop(0, 4, close, 0)
        elif chips == 2:
            visit(member(1, 0))
            visit(member(1, 1))

    def for_peers(visit):
        for_far(visit)
        for_close(visit)
        visit(member(0, 1))

    def matrix_pass(index, matrix_ref):
        here = at_rows(index)
        for x in range(cells):
            weight = 1.0 + look_up(mat_v[x, here, :], table)
            d_v[x, here, :] = 1.0 / weight
            excess = weight * scale
            if x == 0:
                ground = excess
                inverse = 1.0 / (2.0 + ground)
                conductance = inverse
                left_ground = conductance * ground
            elif x < cells - 1:
                ground = excess + carried
                inverse = 1.0 / (conductance + 1.0 + ground)
                conductance = conductance * inverse
                left_ground = left_ground + conductance * ground
            else:
                ground = excess + carried
            if x < cells - 1:
                carried = ground * inverse
                r_v[x, here, :] = inverse
                a_v[x, here, :] = conductance
        matrix_ref[0] = conductance
        matrix_ref[1] = left_ground
        matrix_ref[2] = ground

    table_copy.wait()
    table = [table_ref[k] for k in range(MATS)]
    loads[0].wait()

    def matrix_visit(peer):
        matrix_pass(peer, am_send.at[peer])
        send(am_send.at[peer], am_recv.at[a], am_ss, am_rs, base + peer).start()

    for_close(matrix_visit)
    matrix_visit(member(0, 1))
    matrix_pass(a, am_recv.at[a])
    if chips > 2:
        pl.semaphore_wait(x_token, 1)
    for_far(matrix_visit)

    loads[1].wait()
    loads[2].wait()
    loads[3].wait()

    def velocity_pass(index, _):
        here = at_rows(index)
        after = pl.ds(pl.multiple_of(index * rows_a + rows_a, 8), 8)
        for x in range(cells):
            damping = d_v[x, here, :]
            pressure = p_v[x, here, :]
            upper = pltpu.roll(pressure, rows_a - 1, axis=0)
            upper = jnp.where(row_of == rows_a - 1, p_v[x, after, :][0:1, :], upper)
            vyn_v[x, pl.ds(pl.multiple_of(index * rows_a + 8, 8), rows_a), :] = damping * (
                vy_v[x, here, :] - 0.5 * (upper - pressure))
            beyond = jnp.where(lane_of == lanes - 1, 0.0, pltpu.roll(pressure, lanes - 1, axis=1))
            vzn_v[x, here, :] = damping * (vz_v[x, here, :] - 0.5 * (beyond - pressure))
        return 0

    lax.fori_loop(0, GROUP, velocity_pass, 0)

    for copy in edges:
        copy.wait()

    @pl.when(has_below)
    def _():
        for copy in ups:
            copy.wait_recv()

    @pl.when(has_above)
    def _():
        goes_down.wait_recv()

    own_damping = 1.0 / (1.0 + look_up(edge_mat[...], table))
    above = jnp.where(has_above, halo[2], 0.0)
    last_row = own_damping * (edge[1] - 0.5 * (above - edge[0]))
    below_damping = 1.0 / (1.0 + look_up(halo_mat[...], table))
    below_row = below_damping * (halo[1] - 0.5 * (edge[2] - halo[0]))
    below_row = jnp.where(has_below, below_row, 0.0)
    vyn_v[:, pl.ds(rows_y + 7, 1), :] = last_row
    vyn_v[:, pl.ds(7, 1), :] = below_row

    def source_pass(index, source_ref):
        here = at_rows(index)
        behind = pl.ds(pl.multiple_of(index * rows_a, 8), 8)
        for x in range(cells):
            vyn = vyn_v[x, pl.ds(pl.multiple_of(index * rows_a + 8, 8), rows_a), :]
            lower = pltpu.roll(vyn, 1, axis=0)
            lower = jnp.where(row_of == 0, vyn_v[x, behind, :][7:8, :], lower)
            vzn = vzn_v[x, here, :]
            before = jnp.where(lane_of == 0, 0.0, pltpu.roll(vzn, 1, axis=1))
            source = (p_v[x, here, :] - 0.5 * (vyn - lower + vzn - before)) * scale
            total = source if x == 0 else source + passed
            if x < cells - 1:
                passed = total * r_v[x, here, :]
                tr_v[x, here, :] = passed
                share = total * a_v[x, here, :]
                left_source = share if x == 0 else left_source + share
        source_ref[0] = left_source
        source_ref[1] = total

    def source_visit(peer):
        source_pass(peer, as_send.at[peer])
        send(as_send.at[peer], as_recv.at[a], as_ss, as_rs, base + peer).start()

    for_peers(source_visit)
    source_pass(a, as_recv.at[a])

    if groups > 2:
        @pl.when(z < solver)
        def _():
            pl.semaphore_wait(z_token, 1)

        @pl.when(z < min(half, solver) - 1)
        def _():
            signal(z_token, at_z(1))

        @pl.when((z > half) & (z < solver))
        def _():
            signal(z_token, at_z(-1))

    def to_solver(j, source, target, ss, rs):
        return send(source.at[j], target.at[z], ss, rs, (solver + j) * GROUP + a)

    def hand_up(source, target, ss, rs):
        for j in range(2):
            @pl.when(z != solver + j)
            def _():
                to_solver(j, source, target, ss, rs).start()

            @pl.when(z == solver + j)
            def _():
                target[z] = source[j]

    others = pl.ds(0, GROUP - 1)
    partner = base + member(0, 1)
    all_matrix = send(am_send.at[others], am_recv.at[others], am_ss, am_rs, partner)
    all_source = send(as_send.at[others], as_recv.at[others], as_ss, as_rs, partner)
    all_back = send(da_recv.at[others], da_recv.at[others], da_ss, da_rs.at[0], partner)
    all_matrix.wait_recv()
    segment, tree = build_matrix([tuple(am_recv[k, v] for v in range(3)) for k in range(GROUP)], 0, GROUP)
    for j in range(2):
        for v in range(3):
            bm_send[j, v] = segment[v][rows_b * j:rows_b * (j + 1), :]
    hand_up(bm_send, bm_recv, bm_ss, bm_rs)

    all_source.wait_recv()
    levels = [None] * GROUP
    pair = build_source(tree, [(as_recv[k, 0], as_recv[k, 1]) for k in range(GROUP)], 0, GROUP, levels)
    for j in range(2):
        for v in range(2):
            bs_send[j, v] = pair[v][rows_b * j:rows_b * (j + 1), :]
    hand_up(bs_send, bs_recv, bs_ss, bs_rs)

    def back_b(peer, j):
        return send(nodes_b.at[pl.ds(peer, 2)], db_recv.at[j], db_ss, db_rs.at[j], peer * GROUP + a)

    @pl.when(z >= solver)
    def _():
        j = z - solver
        every = pl.ds(0, groups - 1)
        send(bm_recv.at[every], bm_recv.at[every], bm_ss, bm_rs, at_z(1)).wait_recv()
        whole, tree_b = build_matrix([tuple(bm_recv[k, v] for v in range(3)) for k in range(groups)], 0, groups)
        end_inverse = 1.0 / (whole[0] + (whole[2] + 1.0))
        send(bs_recv.at[every], bs_recv.at[every], bs_ss, bs_rs, at_z(1)).wait_recv()
        levels_b = [None] * groups
        sums = build_source(tree_b, [(bs_recv[k, 0], bs_recv[k, 1]) for k in range(groups)], 0, groups, levels_b)
        values_b = [None] * groups
        nothing = jnp.zeros((rows_b, lanes), jnp.float32)
        values_b[groups - 1] = sums[1] * end_inverse
        spread(tree_b, levels_b, nothing, values_b[groups - 1], values_b)
        nodes_b[0] = nothing
        for k in range(groups):
            nodes_b[k + 1] = values_b[k]
        for k in range(1, groups):
            back_b(lax.rem(z + k, groups), j).start()
        db_recv[j] = nodes_b[pl.ds(z, 2)]

    for j in range(2):
        @pl.when(z != solver + j)
        def _():
            back_b(0, j).wait_recv()

    before_all = jnp.concatenate([db_recv[0, 0], db_recv[1, 0]], axis=0)
    after_all = jnp.concatenate([db_recv[0, 1], db_recv[1, 1]], axis=0)
    values = [None] * GROUP
    values[GROUP - 1] = after_all
    spread(tree, levels, before_all, after_all, values)
    nodes_a[0] = before_all
    for k in range(GROUP):
        nodes_a[k + 1] = values[k]

    def back_a(peer, slot):
        return send(nodes_a.at[pl.ds(peer, 2)], da_recv.at[slot], da_ss, da_rs.at[slot], base + peer)

    def back_start(peer):
        back_a(peer, a).start()

    for_peers(back_start)

    def finish_lines(index, before, after):
        here = at_rows(index)
        q_v[cells - 1, here, :] = after
        for x in range(cells - 2, -1, -1):
            after = tr_v[x, here, :] + r_v[x, here, :] * after + a_v[x, here, :] * before
            q_v[x, here, :] = after

    finish_lines(a, nodes_a[a], nodes_a[a + 1])

    def back_wait(peer):
        back_a(peer, peer).wait_recv()
        finish_lines(peer, da_recv[peer, 0], da_recv[peer, 1])

    back_wait(member(0, 1))
    if chips > 2:
        def close_wait(k, _):
            back_wait(member(1 + 2 * (k % 2), k // 2))
            return 0
        lax.fori_loop(0, 4, close_wait, 0)

        def far_wait(k, _):
            back_wait(member(2, k))
            return 0
        lax.fori_loop(0, 2, far_wait, 0)
    elif chips == 2:
        back_wait(member(1, 0))
        back_wait(member(1, 1))

    @pl.when(has_above)
    def _():
        for copy in ups:
            copy.wait_send()

    @pl.when(has_below)
    def _():
        goes_down.wait_send()

    all_matrix.wait_send()
    all_source.wait_send()
    all_back.wait_send()

    @pl.when(z < solver)
    def _():
        send(bm_send, bm_recv.at[pl.ds(0, 2)], bm_ss, bm_rs, at_z(1)).wait_send()
        send(bs_send, bs_recv.at[pl.ds(0, 2)], bs_ss, bs_rs, at_z(1)).wait_send()

    @pl.when(z >= solver)
    def _():
        every = pl.ds(0, groups - 1)
        send(bm_send.at[0], bm_recv.at[0], bm_ss, bm_rs, at_z(1)).wait_send()
        send(bs_send.at[0], bs_recv.at[0], bs_ss, bs_rs, at_z(1)).wait_send()
        send(bs_recv.at[every], bs_recv.at[every], db_ss, bs_rs, at_z(1)).wait_send()


def finish(vyn_v, vzn_v, q_v, q_out, vy_out, vz_out, out_sem):
    rows_y = vzn_v.shape[1]
    copies = [
        pltpu.make_async_copy(q_v, q_out, out_sem.at[0]),
        pltpu.make_async_copy(vzn_v, vz_out, out_sem.at[1]),
        pltpu.make_async_copy(vyn_v.at[:, pl.ds(8, rows_y), :], vy_out, out_sem.at[2]),
    ]
    for copy in copies:
        copy.start()
    for copy in copies:
        copy.wait()


def solution(mesh):
    groups = mesh.shape["gx"] // GROUP
    columns = mesh.shape["gy"]

    def body(pressure, vel_y, vel_z, material, absorb_table):
        cells, rows_y, lanes = pressure.shape
        rows_a = rows_y // GROUP
        rows_b = rows_a // 2
        f32 = jnp.float32
        vmem = pltpu.VMEM
        dma = pltpu.SemaphoreType.DMA
        kept = [
            vmem((cells, rows_y + 8, lanes), f32),
            vmem((cells, rows_y, lanes), f32),
            vmem((cells, rows_y, lanes), f32),
        ]
        scratch = [
            pltpu.SMEM((MATS,), f32),
            vmem((cells, rows_y + 8, lanes), f32),
            vmem((cells, rows_y, lanes), f32),
            vmem((cells, rows_y, lanes), f32),
            vmem((cells, rows_y, lanes), jnp.int32),
            vmem((cells, rows_y, lanes), f32),
            vmem((cells - 1, rows_y, lanes), f32),
            vmem((cells - 1, rows_y, lanes), f32),
            vmem((cells - 1, rows_y, lanes), f32),
            vmem((3, cells, 1, lanes), f32),
            vmem((cells, 1, lanes), jnp.int32),
            vmem((3, cells, 1, lanes), f32),
            vmem((cells, 1, lanes), jnp.int32),
            vmem((GROUP, 3, rows_a, lanes), f32),
            vmem((GROUP, 3, rows_a, lanes), f32),
            vmem((GROUP, 2, rows_a, lanes), f32),
            vmem((GROUP, 2, rows_a, lanes), f32),
            vmem((2, 3, rows_b, lanes), f32),
            vmem((groups, 3, rows_b, lanes), f32),
            vmem((2, 2, rows_b, lanes), f32),
            vmem((groups, 2, rows_b, lanes), f32),
            vmem((groups + 1, rows_b, lanes), f32),
            vmem((2, 2, rows_b, lanes), f32),
            vmem((GROUP + 1, rows_a, lanes), f32),
            vmem((GROUP, 2, rows_a, lanes), f32),
            dma, dma((4,)), dma((4,)), dma((4,)), dma((4,)),
            dma, dma, dma, dma,
            dma, dma, dma, dma,
            dma, dma((2,)), dma, dma((GROUP,)),
            pltpu.SemaphoreType.REGULAR, pltpu.SemaphoreType.REGULAR,
        ]
        hbm = pl.BlockSpec(memory_space=pltpu.HBM)
        local = pl.BlockSpec(memory_space=pltpu.VMEM)
        held = pl.pallas_call(
            functools.partial(kernel, groups, columns),
            out_shape=kept,
            in_specs=[hbm] * 5,
            out_specs=[local] * len(kept),
            scratch_shapes=scratch,
            compiler_params=pltpu.CompilerParams(collective_id=0, has_side_effects=True, vmem_limit_bytes=LIMIT1),
            name="exchange",
        )(absorb_table, pressure, vel_y, vel_z, material)
        return pl.pallas_call(
            finish,
            out_shape=[jax.ShapeDtypeStruct(pressure.shape, f32)] * 3,
            in_specs=[local] * len(kept),
            out_specs=[hbm] * 3,
            scratch_shapes=[dma((3,))],
            compiler_params=pltpu.CompilerParams(vmem_limit_bytes=LIMIT2),
            name="finish",
        )(*held)

    return jax.shard_map(
        body,
        mesh=mesh,
        in_specs=(P("gx", "gy", None), P("gx", "gy", None), P("gx", "gy", None), P("gx", "gy", None), P()),
        out_specs=(P("gx", "gy", None), P("gx", "gy", None), P("gx", "gy", None)),
        check_vma=False,
    )
```

time: 32.9 us -> 29.8 us (0.906)
  Pallas kernels: 32.1 us -> 29 us
    pallas_call x1, Pallas kernels: 30.9 us -> 27.9 us  [body(): pl.pallas_call(functools.partial(kernel, groups, columns), out_shape=kept...]
where the time goes in v3:
time: 29.8 us; the launch traced here: 29.7 us
  Pallas kernels  29 us (97%)
  between operations  0.64 us (2%)
    pallas_call x1, Pallas kernels, body(): pl.pallas_call(functools.partial(kernel, groups, columns), out_shape=kept...  27.9 us
    pallas_call x1, Pallas kernels, body(): pl.pallas_call(finish, out_shape=[jax.ShapeDtypeStruct(pressure.shape, f3...  1.17 us

profile of v3, /device:TPU:1, one launch (start us, length us, event | category | flops | bytes accessed | tf_op | source)
XLA Modules:
  0.0 29.7 jit_solution(33030406180118610)
XLA Ops:
  0.6 27.9 %exchange.1 = (f32[8,136,128]{2,1,0:T(8,128)S(1)}, f32[8,128,128]{2,1,0:T(8,128)S(1)}, f32[8,128,128]{2,1,0:T(8,128)S(1)}) custom-call(f32[8]{0:T(128)} %table_hbm.1, f32[8,128,128]{2,1,0:T(8,128)} %p_hbm.1, f32[8,128,128]{2,1,0:T(8,128)} %vy_hbm.1, f32[8,128,128]{2,1,0:T(8,128)} %vz_hbm.1, s32[8,128,128]{2,1,0:T(8,128)} %mat_hbm.1), custom_call_target="tpu_custom_call" | custom-call | tf_op jit(solution)/shard_map/exchange/pallas_call | solution.py:531
  28.5 1.2 %finish.1 = (f32[8,128,128]{2,1,0:T(8,128)}, f32[8,128,128]{2,1,0:T(8,128)}, f32[8,128,128]{2,1,0:T(8,128)}) custom-call(f32[8,136,128]{2,1,0:T(8,128)S(1)} %get-tuple-element.6.vyn_v, f32[8,128,128]{2,1,0:T(8,128)S(1)} %get-tuple-element.7.vzn_v, f32[8,128,128]{2,1,0:T(8,128)S(1)} %get-tuple-element.8.q_v), custom_call_target="tpu_custom_call" | custom-call | tf_op jit(solution)/shard_map/finish/pallas_call | solution.py:540
